TPU v7x, 512 devices: a whole 4x8x8 slice. The times are simulated.
512 devices in a mesh: dp: 32 (over x, y), table: 16 (over z, core).
Axes of the slice: x: 4, y: 8, z: 8, core: 2. Of those that a mesh axis runs over, the one named last changes fastest.
Arguments:
- table: bfloat16 [12288, 512], P('table'), may hold values from -6 to 6
- history_shard: int32 [512, 256, 1], P(('dp', 'table')), may hold values from 0 to 15; in each aligned block of 256 rows (0 to 255, 256 to 511, ..., all dimensions but the last counted through in order) at most 32 rows name the same one
- history_row: int32 [512, 256], P(('dp', 'table')), may hold values from 0 to 767
- lengths: int32 [512], P(('dp', 'table')), may hold values from 1 to 256, 98304 in all
- w_in: bfloat16 [512, 2048], replicated, may hold values from -0.25 to 0.25
- w_out: bfloat16 [512, 512], replicated, may hold values from -0.25 to 0.25
- cotangent: bfloat16 [512, 256, 512], P(('dp', 'table')), may hold values from -6 to 6
Outputs:
- table_grad: float32 [12288, 512], P('table')
- dense_grad: bfloat16 [512, 512], replicated
Inputs may be any that keep to these rules, and one draw needn't show every extreme that they name: `history_shard`: among the 256 history slots of one device's samples, at most 32 name one table shard, and that bound is met by some shard in some device's slots. `lengths`: some sample has the full length 256.
All inputs are finite; a program needn't handle non-finite values. No bound on the sum of `lengths` on one device may be relied on, other than what follows from the above.
Results may differ from a plain program's by a relative error of at most 0.017.
Values may be sent and summed in bfloat16 or wider, within the bound.
A program may use at most 64 MiB of HBM per device.

v0:
```python
import math
import jax
import jax.numpy as jnp
from jax import lax
from jax.sharding import PartitionSpec as P

HEADS = 4


def layer_norm(values):
    average = jnp.mean(values, axis=-1, keepdims=True)
    centred = values - average
    variance = jnp.mean(centred * centred, axis=-1, keepdims=True)
    return centred * lax.rsqrt(variance + 1e-06)


def hstu_layer(embedded, w_in, w_out, lengths):
    samples_here, seq_span, model_width = embedded.shape
    head_dim = model_width // HEADS
    normed = layer_norm(embedded.astype(jnp.float32)).astype(jnp.bfloat16)
    projected = jax.nn.silu(
        jnp.dot(
            normed.reshape(samples_here * seq_span, model_width),
            w_in,
            preferred_element_type=jnp.float32,
        )
    )
    gate_part = projected[:, :model_width]
    shaped = (samples_here, seq_span, HEADS, head_dim)
    values = projected[:, model_width : 2 * model_width].astype(jnp.bfloat16).reshape(shaped)
    queries = projected[:, 2 * model_width : 3 * model_width].astype(jnp.bfloat16).reshape(shaped)
    keys = projected[:, 3 * model_width :].astype(jnp.bfloat16).reshape(shaped)
    scores = jnp.einsum(
        "blhd,bmhd->bhlm", queries.astype(jnp.float32), keys.astype(jnp.float32)
    ) * head_dim ** (-0.5)
    positions = jnp.arange(seq_span)
    live_keys = (positions[None, None, :] <= positions[None, :, None]) & (
        positions[None, None, :] < lengths[:, None, None]
    )
    weights = (
        jnp.where(live_keys[:, None], jax.nn.silu(scores), 0.0)
        / lengths.astype(jnp.float32)[:, None, None, None]
    )
    weights = weights.astype(jnp.bfloat16)
    attended = jnp.einsum(
        "bhlm,bmhd->blhd", weights.astype(jnp.float32), values.astype(jnp.float32)
    ).reshape(samples_here * seq_span, model_width)
    mixed = (layer_norm(attended) * gate_part).astype(jnp.bfloat16)
    output = jnp.dot(mixed, w_out, preferred_element_type=jnp.float32) + embedded.reshape(
        -1, model_width
    ).astype(jnp.float32)
    return (output, mixed)


def per_device(table, history_shard, history_row, lengths, w_in, w_out, cotangent):
    shard_rows, model_width = table.shape
    samples_here, seq_span = history_row.shape
    groups = lax.axis_size("table")
    slot_count = samples_here * seq_span
    capacity = 2 * slot_count // groups
    owners = history_shard[:, :, 0].reshape(-1)
    local_rows = history_row.reshape(-1)
    owner_hits = (owners[:, None] == jnp.arange(groups)[None, :]).astype(jnp.int32)
    slot_rank = jnp.sum((jnp.cumsum(owner_hits, axis=0) - owner_hits) * owner_hits, axis=1)
    position = owners * capacity + slot_rank
    requested = (
        jnp.zeros((groups * capacity,), jnp.int32)
        .at[position]
        .set(local_rows)
        .reshape(groups, capacity)
    )
    incoming = lax.all_to_all(requested, "table", split_axis=0, concat_axis=0, tiled=True).reshape(
        -1
    )
    global_rows = owners * shard_rows + local_rows
    piece = lax.all_gather(table, "table", axis=0, tiled=True)
    inside = (global_rows >= 0) & (global_rows < piece.shape[0])
    taken = piece[jnp.clip(global_rows, 0, piece.shape[0] - 1)].astype(jnp.float32)
    embedded = jnp.where(inside[:, None], taken, 0.0).astype(jnp.bfloat16)
    embedded = embedded.reshape(samples_here, seq_span, model_width)
    output, pullback, mixed = jax.vjp(
        lambda rows_in: hstu_layer(rows_in, w_in, w_out, lengths), embedded, has_aux=True
    )
    row_live = jnp.arange(seq_span)[None, :] < lengths[:, None]
    grad_seed = jnp.where(row_live[:, :, None], cotangent, jnp.zeros_like(cotangent))
    flat_seed = grad_seed.reshape(-1, model_width)
    (row_grad,) = pullback(flat_seed.astype(jnp.float32))
    dense_part = jnp.dot(mixed.T, flat_seed, preferred_element_type=jnp.float32)
    outgoing = (
        jnp.zeros((groups * capacity, model_width), jnp.bfloat16)
        .at[position]
        .set(row_grad.reshape(-1, model_width))
    )
    arrived = lax.all_to_all(
        outgoing.reshape(groups, capacity, model_width),
        "table",
        split_axis=0,
        concat_axis=0,
        tiled=True,
    )
    local_grad = (
        jnp.zeros((shard_rows, model_width), jnp.float32)
        .at[incoming]
        .add(arrived.reshape(-1, model_width).astype(jnp.float32))
    )
    total_slots = slot_count * lax.axis_size("dp") * groups
    grad_scale = 1.0 / math.sqrt(total_slots)
    table_grad = lax.psum(local_grad, "dp")
    dense_total = lax.psum(dense_part, ("dp", "table"))
    dense_grad = (dense_total * grad_scale).astype(jnp.bfloat16)
    return (table_grad, dense_grad)


def solution(mesh):
    in_specs = (
        P("table", None),
        P(("dp", "table"), None, None),
        P(("dp", "table"), None),
        P(("dp", "table")),
        P(),
        P(),
        P(("dp", "table"), None, None),
    )
    out_specs = (P("table", None), P())
    return jax.shard_map(
        per_device, mesh=mesh, in_specs=in_specs, out_specs=out_specs, check_vma=False
    )
```

profile of v0, /device:TPU:64, one launch (start us, length us, event | category | flops | bytes accessed | tf_op | source)
XLA Modules:
  0.0 582.9 jit_solution(10138484838293075610)
XLA Ops:
  7.2 0.0 copy-start
  7.2 0.0 all-gather.2.cloned.1.call-start
  7.2 0.7 all-gather.2.cloned.1.call-update
  7.9 0.7 fusion.64
  8.6 0.6 reduce-window.6
  9.2 0.2 slice_reduce_fusion
  9.4 0.8 fusion.63
  10.2 0.7 compare_select_fusion.1
  10.9 1.6 scatter_custom_fusion
  12.4 0.7 all_to_all.9
  13.1 10.0 %all-to-all-start = ((s32[16,1,32]{2,1,0:T(1,128)}), s32[16,1,32]{2,1,0:T(1,128)S(1)}, u32[]{:S(2)}, u32[]{:S(2)}) async-start(s32[16,1,32]{2,1,0:T(1,128)} %all_to_all.9), calls=%async_computation | async-start | bytes 16384 | tf_op jit(solution)/shard_map/all_to_all | solution.py:72
  23.8 0.7 compare_and_fusion
  24.5 66.3 %all-gather.2.cloned.1.call-done = bf16[12288,512]{1,0:T(8,128)(2,1)} async-done(((bf16[768,512]{1,0:T(8,128)(2,1)}), bf16[12288,512]{1,0:T(8,128)(2,1)}) %all-gather.2.cloned.1.call-update) | async-done | bytes 12582928 | tf_op jit(solution)/shard_map/all_gather | solution.py:76
  90.8 7.4 %gather_fusion = bf16[256,512]{1,0:T(8,128)(2,1)S(1)} fusion(bf16[12288,512]{1,0:T(8,128)(2,1)} %all-gather.2.cloned.1.call-done, s32[1024]{0:T(1024)S(1)} %pad_clamp_fusion), kind=kCustom, calls=%fused_computation | custom fusion | bytes 525312 | tf_op jit(solution)/shard_map/gather | solution.py:78
  98.2 0.2 convert_reduce_fusion
  98.4 0.2 fusion.38
  98.6 0.0 copy-done
  98.7 2.8 fusion.76
  101.5 0.8 slice_bitcast_fusion
  102.2 0.1 copy.40
  102.4 0.0 copy-start.4
  102.4 0.1 copy.41
  102.5 0.0 copy-start.6
  102.5 0.0 copy-start.8
  102.5 1.6 divide_convert_fusion
  104.1 0.0 copy-done.4
  104.1 0.0 copy-done.6
  104.1 0.0 copy-done.8
  104.1 0.3 fusion.78
  104.5 0.1 fusion.40
  104.6 0.3 copy-done.2
  104.9 0.2 copy.35
  105.1 1.7 multiply_reduce_fusion.1
  106.9 2.1 fusion.75
  108.9 0.1 broadcast_add_fusion
  109.0 0.1 copy.36
  109.2 0.0 copy-start.5
  109.2 2.0 fusion.26
  111.3 0.2 fusion.80
  111.5 0.0 copy-done.7
  111.5 1.0 fusion.79
  112.5 0.9 fusion.81
  113.5 0.1 copy.37
  113.6 1.8 copy.38
  115.4 1.8 copy.39
  117.2 3.4 multiply_reduce_fusion
  120.6 1.0 fusion.74
  121.6 2.9 scatter_custom_fusion.1
  124.5 0.0 all-to-all-done
  124.5 6.9 %all-to-all-start.1 = ((bf16[16,32,512]{2,1,0:T(8,128)(2,1)}), bf16[16,32,512]{2,1,0:T(8,128)(2,1)}, u32[]{:S(2)}, u32[]{:S(2)}) async-start(bf16[16,32,512]{2,1,0:T(8,128)(2,1)} %bitcast.120), calls=%async_computation.1 | async-start | bytes 1048576 | tf_op jit(solution)/shard_map/all_to_all | solution.py:94
  131.4 0.2 all-reduce.9.cloned.1.call-start
  131.6 2.5 fusion.45
  134.1 0.0 all-reduce.9.cloned.1.call-update
  134.1 0.0 all-reduce.7.cloned.1.call-start
  134.2 0.5 broadcast.379
  134.7 0.7 reduce.15
  135.4 0.1 reshape.502
  135.4 10.4 %all-to-all-done.1 = bf16[16,32,512]{2,1,0:T(8,128)(2,1)} async-done(((bf16[16,32,512]{2,1,0:T(8,128)(2,1)}), bf16[16,32,512]{2,1,0:T(8,128)(2,1)}, u32[]{:S(2)}, u32[]{:S(2)}) %all-to-all-start.1) | async-done | bytes 524320 | tf_op jit(solution)/shard_map/all_to_all | solution.py:94
  145.8 5.5 scatter_custom_fusion.2
  151.3 0.0 all-reduce.7.cloned.1.call-update
  151.3 258.6 %all-reduce.9.cloned.1.call-done = f32[512,512]{1,0:T(8,128)} async-done(((f32[512,512]{1,0:T(8,128)}), f32[512,512]{1,0:T(8,128)}) %all-reduce.9.cloned.1.call-update) | async-done | bytes 1048592 | tf_op jit(solution)/shard_map/psum | solution.py:109
  409.9 2.1 multiply_convert_fusion
  412.0 161.6 %all-reduce.7.cloned.1.call-done = f32[768,512]{1,0:T(8,128)} async-done(((f32[768,512]{1,0:T(8,128)}), f32[768,512]{1,0:T(8,128)}) %all-reduce.7.cloned.1.call-update) | async-done | bytes 1572880 | tf_op jit(solution)/shard_map/psum | solution.py:108
  573.7 2.7 copy.58
  (20 shorter events, 0.2 us)
Async XLA Ops:
  7.2 91.5 %copy-start = (bf16[512,2048]{1,0:T(8,128)(2,1)S(1)}, bf16[512,2048]{1,0:T(8,128)(2,1)}, u32[]{:S(2)}) copy-start(bf16[512,2048]{1,0:T(8,128)(2,1)} %param.11) | copy-start | bytes 6291460
  7.2 83.6 %all-gather.2.cloned.1.call-start = ((), (), s32[]{:S(2)}) async-start(), calls=%async_computation.2 | async-start | bytes 13369344 | tf_op jit(solution)/shard_map/all_gather | solution.py:76
  13.1 111.4 %all-to-all-start = ((s32[16,1,32]{2,1,0:T(1,128)}), s32[16,1,32]{2,1,0:T(1,128)S(1)}, u32[]{:S(2)}, u32[]{:S(2)}) async-start(s32[16,1,32]{2,1,0:T(1,128)} %all_to_all.9), calls=%async_computation | async-start | bytes 16384 | tf_op jit(solution)/shard_map/all_to_all | solution.py:72
  102.4 1.8 copy-start.4
  102.5 1.6 copy-start.6
  102.5 1.6 copy-start.8
  104.1 0.8 copy-start.2
  109.2 2.1 copy-start.5
  109.2 2.3 copy-start.7
  111.2 1.3 copy-start.3
  117.2 4.4 copy-start.1
  124.5 21.3 %all-to-all-start.1 = ((bf16[16,32,512]{2,1,0:T(8,128)(2,1)}), bf16[16,32,512]{2,1,0:T(8,128)(2,1)}, u32[]{:S(2)}, u32[]{:S(2)}) async-start(bf16[16,32,512]{2,1,0:T(8,128)(2,1)} %bitcast.120), calls=%async_computation.1 | async-start | bytes 1048576 | tf_op jit(solution)/shard_map/all_to_all | solution.py:94
  131.4 278.5 %all-reduce.9.cloned.1.call-start = ((), (), s32[]{:S(2)}) async-start(), calls=%async_computation.4 | async-start | bytes 2097152 | tf_op jit(solution)/shard_map/psum | solution.py:109
  134.1 439.6 %all-reduce.7.cloned.1.call-start = ((), (), s32[]{:S(2)}) async-start(), calls=%async_computation.3 | async-start | bytes 3145728 | tf_op jit(solution)/shard_map/psum | solution.py:108
Sparse Core Ops, SparseCore 0:
  10.1 80.5 all-gather.1
  137.3 272.5 all-reduce.8
  414.3 159.3 all-reduce.6
where the time goes:
time: 584 us; the launch traced here: 583 us
  waiting for transfers between devices  498 us (85%)
  local copies, waits for them, and re-layouts  18.5 us (3%)
  other arithmetic  18.5 us (3%)
  starting transfers between devices  17.1 us (3%)
  matrix products  16.5 us (3%)
  between operations  14.6 us (2%)
    psum x1, waiting for transfers between devices, per_device(): dense_total = lax.psum(dense_part, ('dp', 'table'))  259 us
    psum x1, waiting for transfers between devices, per_device(): table_grad = lax.psum(local_grad, 'dp')  162 us
    all_gather x1, waiting for transfers between devices, per_device(): piece = lax.all_gather(table, 'table', axis=0, tiled=True)  66.3 us
  transfers between devices with their start and end apart: 5, of which 4 were waited for; matrix products, arithmetic and copies ran while one was open for 9% of the time, Pallas kernels for 0%

commit v1 on v0

--- a/solution.py
+++ b/solution.py
@@ -73,7 +73,11 @@
         -1
     )
     global_rows = owners * shard_rows + local_rows
-    piece = lax.all_gather(table, "table", axis=0, tiled=True)
+    size = lax.axis_size("table")
+    repeats = [size if d == 0 else 1 for d in range(table.ndim)]
+    piece = lax.all_to_all(
+        jnp.tile(table, repeats), "table", split_axis=0, concat_axis=0, tiled=True
+    )
     inside = (global_rows >= 0) & (global_rows < piece.shape[0])
     taken = piece[jnp.clip(global_rows, 0, piece.shape[0] - 1)].astype(jnp.float32)
     embedded = jnp.where(inside[:, None], taken, 0.0).astype(jnp.bfloat16)

time: 584 us -> 800 us (1.37)
  waiting for transfers between devices: 498 us -> 700 us
    all_to_all x0 -> x1, waiting for transfers between devices: none -> 269 us  [per_device(): lax.all_to_all(jnp.tile(table, repeats), 'table', split_axis=0, concat_ax...]
    all_gather x1 -> x0, waiting for transfers between devices: 66.3 us -> none  [per_device(): piece = lax.all_gather(table, 'table', axis=0, tiled=True)]
    all_to_all x0 -> x1, starting transfers between devices: none -> 10.1 us  [per_device(): lax.all_to_all(jnp.tile(table, repeats), 'table', split_axis=0, concat_ax...]
  transfers between devices with their start and end apart: 5 -> 5, of which waited for: 4 -> 4; matrix products, arithmetic and copies ran while one was open for 9% -> 6% of each run, Pallas kernels for 0% -> 0%
where the time goes in v1:
time: 800 us; the launch traced here: 799 us
  waiting for transfers between devices  700 us (88%)
  local copies, waits for them, and re-layouts  26.2 us (3%)
  starting transfers between devices  23.9 us (3%)
  matrix products  17.5 us (2%)
  other arithmetic  16.5 us (2%)
  between operations  14.9 us (2%)
    all_to_all x1, waiting for transfers between devices, per_device(): lax.all_to_all(jnp.tile(table, repeats), 'table', split_axis=0, concat_ax...  269 us
    psum x1, waiting for transfers between devices, per_device(): dense_total = lax.psum(dense_part, ('dp', 'table'))  259 us
    psum x1, waiting for transfers between devices, per_device(): table_grad = lax.psum(local_grad, 'dp')  162 us
  transfers between devices with their start and end apart: 5, of which 4 were waited for; matrix products, arithmetic and copies ran while one was open for 6% of the time, Pallas kernels for 0%

profile of v1, /device:TPU:64, one launch (start us, length us, event | category | flops | bytes accessed | tf_op | source)
XLA Modules:
  0.0 799.0 jit_solution(3855452248536706553)
XLA Ops:
  7.2 0.0 copy-start
  7.2 7.0 tile.2
  14.2 10.1 %all-to-all-start.1 = ((bf16[16,768,512]{2,1,0:T(8,128)(2,1)}), bf16[16,768,512]{2,1,0:T(8,128)(2,1)}, u32[]{:S(2)}, u32[]{:S(2)}) async-start(bf16[16,768,512]{2,1,0:T(8,128)(2,1)} %tile.2), calls=%async_computation.1 | async-start | bytes 25165824 | tf_op jit(solution)/shard_map/all_to_all | solution.py:78
  24.3 0.0 copy-done.10
  24.3 0.6 reduce-window.6
  24.9 0.2 slice_reduce_fusion
  25.1 0.1 fusion.63
  25.2 0.0 copy-done.11
  25.2 1.4 scatter_custom_fusion
  26.6 0.7 all_to_all.15
  28.0 269.0 %all-to-all-done.1 = bf16[16,768,512]{2,1,0:T(8,128)(2,1)} async-done(((bf16[16,768,512]{2,1,0:T(8,128)(2,1)}), bf16[16,768,512]{2,1,0:T(8,128)(2,1)}, u32[]{:S(2)}, u32[]{:S(2)}) %all-to-all-start.1) | async-done | bytes 12582944 | tf_op jit(solution)/shard_map/all_to_all | solution.py:78
  297.0 6.2 all-to-all-start
  303.3 7.4 gather_fusion
  310.7 0.2 convert_reduce_fusion
  310.9 0.2 fusion.38
  311.1 0.0 copy-done
  311.1 2.8 fusion.76
  314.0 0.8 slice_bitcast_fusion
  314.7 0.1 copy.40
  314.9 0.0 copy-start.4
  314.9 0.1 copy.41
  315.0 0.0 copy-start.6
  315.0 0.0 copy-start.9
  315.1 1.6 divide_convert_fusion
  316.6 0.3 fusion.78
  317.0 0.4 copy-done.2
  317.4 0.2 copy.35
  317.6 0.1 fusion.40
  317.7 1.7 multiply_reduce_fusion.1
  319.5 2.1 fusion.75
  321.6 0.8 broadcast_add_fusion
  322.4 1.8 copy.36
  324.2 1.9 fusion.81
  326.1 2.1 fusion.26
  328.2 0.0 copy-done.7
  328.2 0.0 copy-start.8
  328.2 0.3 fusion.79
  328.5 0.0 copy-done.5
  328.6 0.9 fusion.80
  329.5 0.0 copy-done.8
  329.5 0.8 copy.39
  330.3 0.8 copy.38
  331.2 1.1 copy.37
  332.3 0.0 copy-start.1
  332.3 3.4 multiply_reduce_fusion
  335.7 1.0 fusion.74
  336.7 0.0 copy-done.1
  336.7 2.9 scatter_custom_fusion.1
  339.6 0.0 all-to-all-done
  339.6 7.2 all-to-all-start.2
  346.8 0.0 all-reduce.9.cloned.1.call-start
  346.9 2.5 fusion.45
  349.4 0.0 all-reduce.9.cloned.1.call-update
  349.4 0.3 all-reduce.7.cloned.1.call-start
  349.7 0.5 broadcast.382
  350.2 0.7 reduce.15
  350.9 0.1 reshape.509
  350.9 10.4 %all-to-all-done.2 = bf16[16,32,512]{2,1,0:T(8,128)(2,1)} async-done(((bf16[16,32,512]{2,1,0:T(8,128)(2,1)}), bf16[16,32,512]{2,1,0:T(8,128)(2,1)}, u32[]{:S(2)}, u32[]{:S(2)}) %all-to-all-start.2) | async-done | bytes 524320 | tf_op jit(solution)/shard_map/all_to_all | solution.py:98
  361.3 5.5 scatter_custom_fusion.2
  366.8 0.0 all-reduce.7.cloned.1.call-update
  366.8 259.0 %all-reduce.9.cloned.1.call-done = f32[512,512]{1,0:T(8,128)} async-done(((f32[512,512]{1,0:T(8,128)}), f32[512,512]{1,0:T(8,128)}) %all-reduce.9.cloned.1.call-update) | async-done | bytes 1048592 | tf_op jit(solution)/shard_map/psum | solution.py:113
  625.8 2.1 multiply_convert_fusion
  627.9 161.6 %all-reduce.7.cloned.1.call-done = f32[768,512]{1,0:T(8,128)} async-done(((f32[768,512]{1,0:T(8,128)}), f32[768,512]{1,0:T(8,128)}) %all-reduce.7.cloned.1.call-update) | async-done | bytes 1572880 | tf_op jit(solution)/shard_map/psum | solution.py:112
  789.5 2.7 copy.58
  (26 shorter events, 0.2 us)
Async XLA Ops:
  7.2 304.0 %copy-start = (bf16[512,2048]{1,0:T(8,128)(2,1)S(1)}, bf16[512,2048]{1,0:T(8,128)(2,1)}, u32[]{:S(2)}) copy-start(bf16[512,2048]{1,0:T(8,128)(2,1)} %param.11) | copy-start | bytes 6291460
  14.1 10.1 %copy-start.10 = (s32[1,256,1]{1,2,0:T(1,128)S(1)}, s32[1,256,1]{1,2,0:T(1,128)}, u32[]{:S(2)}) copy-start(s32[1,256,1]{1,2,0:T(1,128)} %param.8) | copy-start | bytes 3076
  14.2 11.0 %copy-start.11 = (s32[1,256]{1,0:T(1,128)S(1)}, s32[1,256]{1,0:T(1,128)}, u32[]{:S(2)}) copy-start(s32[1,256]{1,0:T(1,128)} %param.9) | copy-start | bytes 3076
  14.2 282.9 %all-to-all-start.1 = ((bf16[16,768,512]{2,1,0:T(8,128)(2,1)}), bf16[16,768,512]{2,1,0:T(8,128)(2,1)}, u32[]{:S(2)}, u32[]{:S(2)}) async-start(bf16[16,768,512]{2,1,0:T(8,128)(2,1)} %tile.2), calls=%async_computation.1 | async-start | bytes 25165824 | tf_op jit(solution)/shard_map/all_to_all | solution.py:78
  297.0 42.6 %all-to-all-start = ((s32[16,1,32]{2,1,0:T(1,128)}), s32[16,1,32]{2,1,0:T(1,128)S(1)}, u32[]{:S(2)}, u32[]{:S(2)}) async-start(s32[16,1,32]{2,1,0:T(1,128)} %all_to_all.15), calls=%async_computation | async-start | bytes 16384 | tf_op jit(solution)/shard_map/all_to_all | solution.py:72
  314.9 1.7 copy-start.4
  315.0 1.6 copy-start.6
  315.0 1.6 copy-start.9
  316.6 0.8 copy-start.2
  319.4 4.8 copy-start.3
  326.1 2.1 copy-start.7
  326.1 2.4 copy-start.5
  328.2 1.3 copy-start.8
  332.3 4.4 copy-start.1
  339.6 21.7 %all-to-all-start.2 = ((bf16[16,32,512]{2,1,0:T(8,128)(2,1)}), bf16[16,32,512]{2,1,0:T(8,128)(2,1)}, u32[]{:S(2)}, u32[]{:S(2)}) async-start(bf16[16,32,512]{2,1,0:T(8,128)(2,1)} %bitcast.121), calls=%async_computation.2 | async-start | bytes 1048576 | tf_op jit(solution)/shard_map/all_to_all | solution.py:98
  346.8 278.9 %all-reduce.9.cloned.1.call-start = ((), (), s32[]{:S(2)}) async-start(), calls=%async_computation.4 | async-start | bytes 2097152 | tf_op jit(solution)/shard_map/psum | solution.py:113
  349.4 440.1 %all-reduce.7.cloned.1.call-start = ((), (), s32[]{:S(2)}) async-start(), calls=%async_computation.3 | async-start | bytes 3145728 | tf_op jit(solution)/shard_map/psum | solution.py:112
Sparse Core Ops, SparseCore 0:
  352.7 272.9 all-reduce.8
  630.1 159.3 all-reduce.6
